TPU v7x, 32 devices: a whole 2x2x4 slice. The times are simulated.
32 devices in a mesh: gx: 2 (over x), gy: 4 (over z), gz: 4 (over y, core).
Axes of the slice: x: 2, y: 2, z: 4, core: 2. Of those that a mesh axis runs over, the one named last changes fastest.
Arguments:
- pressure_zero: float32 [32, 64, 1024], P('gx', 'gy', 'gz'), may hold values from -1.2 to 1.2
- pressure_one: float32 [32, 64, 1024], P('gx', 'gy', 'gz'), may hold values from -1.2 to 1.2
- adjoint_upper: float32 [32, 64, 1024], P('gx', 'gy', 'gz'), may hold values from -6 to 6
- adjoint_top: float32 [32, 64, 1024], P('gx', 'gy', 'gz'), may hold values from -6 to 6
- courant_factor: float32 [32, 64, 1024], P('gx', 'gy', 'gz'), may hold values from 0.08 to 0.19
- residual: float32 [4, 1024], P(None, 'gz'), may hold values from -6 to 6
- receiver_cell: int32 [3, 1024], replicated, may hold values from 4 to 1019, as said below
- tap_offset: int32 [3, 16, 1024], replicated, may hold values from -4 to 4
- tap_weight: float32 [16, 1024], replicated, may hold values from -3 to 3
- trace_receiver: int32 [1024], replicated, may hold values from 0 to 1023, each once
Outputs:
- gradient: float32 [32, 64, 1024], P('gx', 'gy', 'gz')
- adjoint_one: float32 [32, 64, 1024], P('gx', 'gy', 'gz')
- adjoint_zero: float32 [32, 64, 1024], P('gx', 'gy', 'gz')
Inputs may be any that keep to these rules, and one draw needn't show every extreme that they name: `receiver_cell`: coordinate 0 of a receiver cell lies in 4 to 27, coordinate 1 in 4 to 59, coordinate 2 in 4 to 1019.
All inputs are finite; a program needn't handle non-finite values.
Results may differ from a plain program's by a relative error of at most 0.00002.
Values sent between devices are 32-bit elements; how exact they have to be, the bound alone decides.
A program may use at most 128 MiB of HBM per device.

v0:
```python
import functools

import jax
import jax.numpy as jnp
import ml_dtypes
import numpy as np
from jax import lax
from jax.experimental import pallas as pl
from jax.experimental.pallas import tpu as pltpu
from jax.sharding import PartitionSpec as P

C = (-205.0 / 72.0, 8.0 / 5.0, -1.0 / 5.0, 8.0 / 315.0, -1.0 / 560.0)
AXES = ("gx", "gy", "gz")
MESH = pl.DeviceIdType.MESH


def split3(v):
    hi = v.astype(jnp.bfloat16)
    rest = v - hi.astype(jnp.float32)
    mid = rest.astype(jnp.bfloat16)
    lo = (rest - mid.astype(jnp.float32)).astype(jnp.bfloat16)
    return [hi, mid, lo]


def nt(a, b):
    return lax.dot_general(a, b, (((1,), (1,)), ((), ())), preferred_element_type=jnp.float32)


def source_kernel(block, res_ref, cell_ref, off_ref, w_ref, tr_ref, out_ref, table, info):
    bx, by, bz = block
    starts = [lax.axis_index(a) * n for a, n in zip(AXES, block)]
    taps, mics = w_ref.shape
    steps = res_ref.shape[0]
    rel = [cell_ref[d : d + 1, :] - starts[d] for d in range(3)]
    near = functools.reduce(
        jnp.logical_and, [(rel[d] >= -4) & (rel[d] < block[d] + 4) for d in range(3)]
    )
    at = [rel[d] + off_ref[d] for d in range(3)]
    inside = functools.reduce(
        jnp.logical_and, [(at[d] >= 0) & (at[d] < block[d]) for d in range(3)]
    )
    row = jnp.where(inside, at[0] * by + at[1], -1)
    col = jnp.where(inside, at[2], -1)
    table[0:taps, :] = row.astype(jnp.float32).astype(jnp.bfloat16)
    table[taps : 2 * taps, :] = col.astype(jnp.float32).astype(jnp.bfloat16)
    for i, part in enumerate(split3(w_ref[...])):
        table[(2 + i) * taps : (3 + i) * taps, :] = part
    near_f = jnp.where(near, 1.0, 0.0)
    lanes = 128
    blocks = mics // lanes
    tri = (
        lax.broadcasted_iota(jnp.int32, (lanes, lanes), 0)
        < lax.broadcasted_iota(jnp.int32, (lanes, lanes), 1)
    )
    tri = jnp.where(tri, 1.0, 0.0).astype(jnp.bfloat16)
    base = jnp.float32(0.0)
    for i in range(blocks):
        part = near_f[:, i * lanes : (i + 1) * lanes]
        before = jnp.dot(
            jnp.broadcast_to(part, (8, lanes)).astype(jnp.bfloat16),
            tri,
            preferred_element_type=jnp.float32,
        )[0:1]
        slot = jnp.where(part > 0.5, before + base, -1.0)
        info[0:1, i * lanes : (i + 1) * lanes] = slot
        base = base + jnp.sum(part)
    count = base.astype(jnp.int32)
    out_ref[...] = jnp.zeros_like(out_ref)

    def chunk(j, carry):
        slots = (lax.broadcasted_iota(jnp.int32, (lanes, mics), 0) + j * lanes).astype(jnp.float32)
        sel = jnp.where(slots == info[0:1, :], 1.0, 0.0)
        mic_id = lax.broadcasted_iota(jnp.int32, (1, mics), 1).astype(jnp.float32)
        mic = jnp.sum(sel * (mic_id + 1.0), axis=1, keepdims=True) - 1.0
        sel_r = jnp.where(tr_ref[...].astype(jnp.float32) == mic, 1.0, 0.0).astype(jnp.bfloat16)
        tab = nt(table[...], sel.astype(jnp.bfloat16))
        rows = tab[0:taps]
        cols = tab[taps : 2 * taps]
        weights = tab[2 * taps : 3 * taps] + tab[3 * taps : 4 * taps] + tab[4 * taps : 5 * taps]
        res = sum(nt(part, sel_r) for part in split3(res_ref[...]))
        iota_row = lax.broadcasted_iota(jnp.int32, (bx * by, lanes), 0).astype(jnp.float32)
        iota_col = lax.broadcasted_iota(jnp.int32, (bz, lanes), 0).astype(jnp.float32)
        group = 4
        for t0 in range(0, taps, group):
            left, right = [[] for _ in range(steps)], []
            for t in range(t0, t0 + group):
                row_hot = iota_row == rows[t : t + 1]
                col_hot = jnp.where(iota_col == cols[t : t + 1], 1.0, 0.0).astype(jnp.bfloat16)
                right += [col_hot, col_hot]
                for n in range(steps):
                    amount = weights[t : t + 1] * res[n : n + 1]
                    hi = amount.astype(jnp.bfloat16).astype(jnp.float32)
                    lo = amount - hi
                    left[n].append(jnp.where(row_hot, hi, 0.0).astype(jnp.bfloat16))
                    left[n].append(jnp.where(row_hot, lo, 0.0).astype(jnp.bfloat16))
            right = jnp.concatenate(right, axis=1)
            for n in range(steps):
                out_ref[n] += nt(jnp.concatenate(left[n], axis=1), right)
        return carry

    lax.fori_loop(0, (count + lanes - 1) // lanes, chunk, 0)


def build_sources(block, residual, receiver_cell, tap_offset, tap_weight, trace_receiver):
    steps = residual.shape[0]
    taps, mics = tap_weight.shape
    return pl.pallas_call(
        functools.partial(source_kernel, block),
        out_shape=jax.ShapeDtypeStruct((steps, block[0] * block[1], block[2]), jnp.float32),
        in_specs=[pl.BlockSpec(memory_space=pltpu.VMEM)] * 5,
        out_specs=pl.BlockSpec(memory_space=pltpu.VMEM),
        scratch_shapes=[
            pltpu.VMEM((5 * taps, mics), jnp.bfloat16),
            pltpu.VMEM((8, mics), jnp.float32),
        ],
        compiler_params=pltpu.CompilerParams(vmem_limit_bytes=40 * 2**20),
        name="sources",
    )(residual, receiver_cell, tap_offset, tap_weight, trace_receiver.reshape(1, mics))


def matrices(nx, ny, nz):
    weight = {k: round(5040 * C[abs(k)]) if k else 0 for k in range(-4, 5)}
    at = np.vectorize(lambda k: weight.get(int(k), 0))
    x, y = np.divmod(np.arange(nx * ny), ny)
    dx, dy = x[:, None] - x[None, :], y[:, None] - y[None, :]
    inner = at(dx) * (dy == 0) + at(dy) * (dx == 0)
    fx, fy = np.divmod(np.arange(4 * ny), ny)
    tile, sub = np.divmod(np.arange(4 * nx), 8)
    lo_x = tile + np.where(sub >= 4, 0, nx // 2)
    hi_x = tile + np.where(sub < 4, 0, nx // 2)
    face_x = np.concatenate([fx - 4, fx + nx, lo_x, hi_x])
    face_y = np.concatenate([fy, fy, sub % 4 - 4, sub % 4 + ny])
    dx, dy = x[:, None] - face_x[None, :], y[:, None] - face_y[None, :]
    faces = at(dx) * (dy == 0) + at(dy) * (dx == 0)
    z = np.arange(nz)
    along = at(z[:, None] - z[None, :])
    end = np.arange(128)
    end = np.where(end < 64, end + nz, end - 128)
    ends = at(end[:, None] - z[None, :])
    return [m.astype(ml_dtypes.bfloat16) for m in (inner, faces, along, ends)]


def nn(a, b):
    return jnp.dot(a, b, preferred_element_type=jnp.float32)


def wave_kernel(
    sizes, ny, p0, p1, q5, q4, cf, src, m_in, m_face, m_z, m_end, grad, one, zero,
    fp, fq, lap, lq, qb, hl, zl, ys, send_sem, recv_sem,
):
    steps = src.shape[0]
    rows, nz = p0.shape
    nx = rows // ny
    faces_rows = (4 * ny, 4 * ny, 4 * nx, 4 * nx)
    me = [lax.axis_index(a) for a in AXES]
    has = []
    for d in range(3):
        has += [me[d] > 0, me[d] < sizes[d] - 1]
    to = []
    for d in range(3):
        to += [{AXES[d]: jnp.maximum(me[d] - 1, 0)}, {AXES[d]: jnp.minimum(me[d] + 1, sizes[d] - 1)}]

    barrier = pltpu.get_barrier_semaphore()
    for f in range(6):
        @pl.when(has[f])
        def _(f=f):
            pl.semaphore_signal(barrier, inc=1, device_id=to[f], device_id_type=MESH)
    pl.semaphore_wait(barrier, sum(h.astype(jnp.int32) for h in has))

    sub = lax.broadcasted_iota(jnp.int32, (8, nz), 0)
    lane = lax.broadcasted_iota(jnp.int32, (rows, 128), 1)

    def field(ch, r):
        if r == 0 and ch == 0:
            return p1
        return (fp, fq)[ch].at[r]

    def landing(ch, r, f):
        if f >= 4:
            return zl.at[ch, r, f - 4]
        return hl.at[ch, r, pl.ds(sum(faces_rows[:f]), faces_rows[f])]

    def copies(ch, r):
        f_ref = field(ch, r)
        srcs = [
            f_ref.at[pl.ds(0, 4 * ny)],
            f_ref.at[pl.ds(rows - 4 * ny, 4 * ny)],
            ys.at[ch, r, 0],
            ys.at[ch, r, 1],
            f_ref.at[pl.ds(0, rows), pl.ds(0, 128)],
            f_ref.at[pl.ds(0, rows), pl.ds(nz - 128, 128)],
        ]
        return [
            pltpu.make_async_remote_copy(
                src_ref=srcs[f],
                dst_ref=landing(ch, r, f ^ 1),
                send_sem=send_sem.at[ch, r, f],
                recv_sem=recv_sem.at[ch, r, f ^ 1],
                device_id=to[f],
                device_id_type=MESH,
            )
            for f in range(6)
        ]

    def send(ch, r):
        f_ref = field(ch, r)
        moves = copies(ch, r)
        for f in (0, 1, 4, 5):
            @pl.when(has[f])
            def _(f=f):
                moves[f].start()
        for i in range(nx // 2):
            lo, far = i * ny, (i + nx // 2) * ny
            a, b = f_ref[lo : lo + 8], f_ref[far : far + 8]
            ys[ch, r, 0, 8 * i : 8 * i + 8] = jnp.where(sub < 4, a, pltpu.roll(b, 4, 0))
            a, b = f_ref[lo + ny - 8 : lo + ny], f_ref[far + ny - 8 : far + ny]
            ys[ch, r, 1, 8 * i : 8 * i + 8] = jnp.where(sub >= 4, a, pltpu.roll(b, 4, 0))
        for f in (2, 3):
            @pl.when(has[f])
            def _(f=f):
                moves[f].start()

    def land(ch, r):
        for f in range(6):
            @pl.when(has[f])
            def _(f=f):
                dst = landing(ch, r, f)
                pltpu.make_async_remote_copy(
                    src_ref=dst, dst_ref=dst,
                    send_sem=send_sem.at[ch, r, f], recv_sem=recv_sem.at[ch, r, f],
                    device_id=to[f], device_id_type=MESH,
                ).wait_recv()

    def local(ch, r, out):
        f = field(ch, r)[...]
        acc = 0.0
        for part in split3(f):
            acc = acc + nn(m_in[...], part) + nn(part, m_z[...])
        out[...] = acc * (1.0 / 5040.0) + (3.0 * C[0]) * f

    def finish(ch, r, out):
        land(ch, r)
        acc = 0.0
        for part in split3(hl[ch, r]):
            acc = acc + nn(m_face[...], part)
        for part in split3(jnp.where(lane < 64, zl[ch, r, 1], zl[ch, r, 0])):
            acc = acc + nn(part, m_end[...])
        return out[...] + acc * (1.0 / 5040.0)

    send(0, 0)
    fq[0] = cf[...] * q4[...]
    send(1, 0)
    for f in range(6):
        @pl.when(jnp.logical_not(has[f]))
        def _(f=f):
            for ch in range(2):
                for r in range(steps):
                    dst = landing(ch, r, f)
                    dst[...] = jnp.zeros(dst.shape, jnp.float32)

    local(0, 0, lap.at[0])
    local(1, 0, lq)
    for r in range(steps):
        full = finish(0, r, lap.at[r])
        lap[r] = full
        if r + 1 < steps:
            old = p0 if r == 0 else field(0, r - 1)
            fp[r + 1] = 2.0 * field(0, r)[...] - old[...] + cf[...] * full
            send(0, r + 1)
            local(0, r + 1, lap.at[r + 1])

        full = finish(1, r, lq)
        now = q4 if r == 0 else qb.at[r - 1]
        old = q5 if r == 0 else (q4 if r == 1 else qb.at[r - 2])
        new = 2.0 * now[...] - old[...] + full + src[steps - 1 - r]
        if r + 1 < steps:
            qb[r] = new
            fq[r + 1] = cf[...] * new
            send(1, r + 1)
            local(1, r + 1, lq)
        else:
            zero[...] = new
            one[...] = now[...]
            total = q4[...] * lap[steps - 1]
            for n in range(1, steps):
                total = total + qb[n - 1] * lap[steps - 1 - n]
            grad[...] = total

    for ch in range(2):
        for r in range(steps):
            moves = copies(ch, r)
            for f in range(6):
                @pl.when(has[f])
                def _(f=f):
                    moves[f].wait_send()


def wave(sizes, p0, p1, q5, q4, cf, src):
    nx, ny, nz = p0.shape
    steps = src.shape[0]
    rows = nx * ny
    f32 = jnp.float32
    flat = [a.reshape(rows, nz) for a in (p0, p1, q5, q4, cf)]
    outs = pl.pallas_call(
        functools.partial(wave_kernel, sizes, ny),
        out_shape=[jax.ShapeDtypeStruct((rows, nz), f32)] * 3,
        in_specs=[pl.BlockSpec(memory_space=pltpu.VMEM)] * 10,
        out_specs=[pl.BlockSpec(memory_space=pltpu.VMEM)] * 3,
        scratch_shapes=[
            pltpu.VMEM((steps, rows, nz), f32),
            pltpu.VMEM((steps, rows, nz), f32),
            pltpu.VMEM((steps, rows, nz), f32),
            pltpu.VMEM((rows, nz), f32),
            pltpu.VMEM((steps, rows, nz), f32),
            pltpu.VMEM((2, steps, 8 * (nx + ny), nz), f32),
            pltpu.VMEM((2, steps, 2, rows, 128), f32),
            pltpu.VMEM((2, steps, 2, 4 * nx, nz), f32),
            pltpu.SemaphoreType.DMA((2, steps, 6)),
            pltpu.SemaphoreType.DMA((2, steps, 6)),
        ],
        compiler_params=pltpu.CompilerParams(
            collective_id=0, has_side_effects=True, vmem_limit_bytes=48 * 2**20
        ),
        name="wave",
    )(*flat, src, *matrices(nx, ny, nz))
    return [o.reshape(nx, ny, nz) for o in outs]


def shards(sizes, p0, p1, q5, q4, cf, residual, receiver_cell, tap_offset, tap_weight, trace_receiver):
    gathered = lax.all_gather(residual, "gz", axis=1, tiled=True)
    src = build_sources(p0.shape, gathered, receiver_cell, tap_offset, tap_weight, trace_receiver)
    return tuple(wave(sizes, p0, p1, q5, q4, cf, src))


def solution(mesh):
    field = P(*AXES)
    return jax.shard_map(
        functools.partial(shards, tuple(mesh.shape[a] for a in AXES)),
        mesh=mesh,
        in_specs=(field,) * 5 + (P(None, "gz"), P(), P(), P(), P()),
        out_specs=(field,) * 3,
        check_vma=False,
    )
```

profile of v0, /device:TPU:1, one launch (start us, length us, event | category | flops | bytes accessed | tf_op | source)
XLA Modules:
  0.0 43.0 jit_solution(11544899713768871713)
XLA Ops:
  0.6 0.0 copy-start.11
  0.6 0.0 copy-start.12
  0.7 6.2 %all_gather.3.res_ref = f32[4,1024]{1,0:T(4,128)S(1)} all-gather(f32[4,256]{1,0:T(4,128)} %param.19), channel_id=1, replica_groups=mesh['gx'=2,'gy'=4,'gz'=4] {'gz'}, dimensions={1}, use_global_device_ids=true | all-gather | bytes 20480 | tf_op jit(solution)/shard_map/all_gather | solution.py:330
  6.9 0.0 copy-done.11
  6.9 0.0 copy-done.12
  6.9 0.0 copy-start.5
  6.9 0.9 %copy-done.5 = s32[3,16,1024]{2,1,0:T(8,128)S(1)} copy-done((s32[3,16,1024]{2,1,0:T(8,128)S(1)}, s32[3,16,1024]{2,1,0:T(8,128)}, u32[]{:S(2)}) %copy-start.5) | copy-done | bytes 196632
  7.8 0.0 copy-start.10
  7.8 0.8 %copy-done.10 = f32[16,1024]{1,0:T(8,128)S(1)} copy-done((f32[16,1024]{1,0:T(8,128)S(1)}, f32[16,1024]{1,0:T(8,128)}, u32[]{:S(2)}) %copy-start.10) | copy-done | bytes 65560
  8.6 0.0 copy-start
  8.6 0.0 copy-start.1
  8.6 0.0 copy-start.2
  8.6 0.0 copy-start.3
  8.6 0.0 copy-start.4
  8.7 3.4 %sources.1.src = f32[4,256,256]{2,1,0:T(8,128)S(1)} custom-call(f32[4,1024]{1,0:T(4,128)S(1)} %all_gather.3.res_ref, s32[3,1024]{1,0:T(4,128)S(1)} %copy-done.11, s32[3,16,1024]{2,1,0:T(8,128)S(1)} %copy-done.5, f32[16,1024]{1,0:T(8,128)S(1)} %copy-done.10, s32[1,1024]{1,0:T(1,128)S(1)} %bitcast.17), custom_call_target="tpu_custom_call" | custom-call | tf_op jit(solution)/shard_map/sources/pallas_call | solution.py:107
  12.1 0.0 copy-done
  12.1 0.0 copy-done.1
  12.1 0.0 copy-done.2
  12.1 0.0 copy-done.3
  12.1 0.0 copy-done.4
  12.1 0.0 copy-start.6
  12.1 0.9 %copy-done.6 = bf16[256,256]{1,0:T(8,128)(2,1)S(1)} copy-done((bf16[256,256]{1,0:T(8,128)(2,1)S(1)}, bf16[256,256]{1,0:T(8,128)(2,1)}, u32[]{:S(2)}) %copy-start.6) | copy-done | bytes 131096
  13.0 0.0 copy-start.7
  13.0 0.9 %copy-done.7 = bf16[256,256]{1,0:T(8,128)(2,1)S(1)} copy-done((bf16[256,256]{1,0:T(8,128)(2,1)S(1)}, bf16[256,256]{1,0:T(8,128)(2,1)}, u32[]{:S(2)}) %copy-start.7) | copy-done | bytes 131096
  13.9 0.0 copy-start.8
  13.9 0.9 %copy-done.8 = bf16[256,256]{1,0:T(8,128)(2,1)S(1)} copy-done((bf16[256,256]{1,0:T(8,128)(2,1)S(1)}, bf16[256,256]{1,0:T(8,128)(2,1)}, u32[]{:S(2)}) %copy-start.8) | copy-done | bytes 131096
  14.8 0.0 copy-start.9
  14.8 0.8 %copy-done.9 = bf16[128,256]{1,0:T(8,128)(2,1)S(1)} copy-done((bf16[128,256]{1,0:T(8,128)(2,1)S(1)}, bf16[128,256]{1,0:T(8,128)(2,1)}, u32[]{:S(2)}) %copy-start.9) | copy-done | bytes 65560
  15.7 25.2 %wave.1 = (f32[256,256]{1,0:T(8,128)S(1)}, f32[256,256]{1,0:T(8,128)S(1)}, f32[256,256]{1,0:T(8,128)S(1)}) custom-call(f32[256,256]{1,0:T(8,128)S(1)} %bitcast.12, f32[256,256]{1,0:T(8,128)S(1)} %bitcast.13, f32[256,256]{1,0:T(8,128)S(1)} %bitcast.14, f32[256,256]{1,0:T(8,128)S(1)} %bitcast.15, f32[256,256]{1,0:T(8,128)S(1)} %bitcast.16, ...), custom_call_target="tpu_custom_call" | custom-call | tf_op jit(solution)/shard_map/wave/pallas_call | solution.py:304
  40.9 0.7 %copy.20 = f32[16,16,256]{2,1,0:T(8,128)} copy(f32[16,16,256]{2,1,0:T(8,128)S(1)} %bitcast.11) | data formatting | bytes 524288
  41.6 0.7 %copy.21 = f32[16,16,256]{2,1,0:T(8,128)} copy(f32[16,16,256]{2,1,0:T(8,128)S(1)} %bitcast.10) | data formatting | bytes 524288
  42.3 0.7 %copy.22 = f32[16,16,256]{2,1,0:T(8,128)} copy(f32[16,16,256]{2,1,0:T(8,128)S(1)} %bitcast.9) | data formatting | bytes 524288
Async XLA Ops:
  0.6 6.2 %copy-start.11 = (s32[3,1024]{1,0:T(4,128)S(1)}, s32[3,1024]{1,0:T(4,128)}, u32[]{:S(2)}) copy-start(s32[3,1024]{1,0:T(4,128)} %cell_ref.1) | copy-start | bytes 36868
  0.6 6.2 %copy-start.12 = (s32[1024]{0:T(1024)S(1)}, s32[1024]{0:T(1024)}, u32[]{:S(2)}) copy-start(s32[1024]{0:T(1024)} %param.23) | copy-start | bytes 12292
  6.9 0.9 %copy-start.5 = (s32[3,16,1024]{2,1,0:T(8,128)S(1)}, s32[3,16,1024]{2,1,0:T(8,128)}, u32[]{:S(2)}) copy-start(s32[3,16,1024]{2,1,0:T(8,128)} %off_ref.1) | copy-start | bytes 589828
  7.8 0.8 %copy-start.10 = (f32[16,1024]{1,0:T(8,128)S(1)}, f32[16,1024]{1,0:T(8,128)}, u32[]{:S(2)}) copy-start(f32[16,1024]{1,0:T(8,128)} %w_ref.1) | copy-start | bytes 196612
  8.6 3.4 %copy-start = (f32[16,16,256]{2,1,0:T(8,128)S(1)}, f32[16,16,256]{2,1,0:T(8,128)}, u32[]{:S(2)}) copy-start(f32[16,16,256]{2,1,0:T(8,128)} %param.14) | copy-start | bytes 786436
  8.6 3.4 %copy-start.1 = (f32[16,16,256]{2,1,0:T(8,128)S(1)}, f32[16,16,256]{2,1,0:T(8,128)}, u32[]{:S(2)}) copy-start(f32[16,16,256]{2,1,0:T(8,128)} %param.15) | copy-start | bytes 786436
  8.6 3.4 %copy-start.2 = (f32[16,16,256]{2,1,0:T(8,128)S(1)}, f32[16,16,256]{2,1,0:T(8,128)}, u32[]{:S(2)}) copy-start(f32[16,16,256]{2,1,0:T(8,128)} %param.16) | copy-start | bytes 786436
  8.6 3.4 %copy-start.3 = (f32[16,16,256]{2,1,0:T(8,128)S(1)}, f32[16,16,256]{2,1,0:T(8,128)}, u32[]{:S(2)}) copy-start(f32[16,16,256]{2,1,0:T(8,128)} %param.17) | copy-start | bytes 786436
  8.6 3.5 %copy-start.4 = (f32[16,16,256]{2,1,0:T(8,128)S(1)}, f32[16,16,256]{2,1,0:T(8,128)}, u32[]{:S(2)}) copy-start(f32[16,16,256]{2,1,0:T(8,128)} %param.18) | copy-start | bytes 786436
  12.1 0.9 %copy-start.6 = (bf16[256,256]{1,0:T(8,128)(2,1)S(1)}, bf16[256,256]{1,0:T(8,128)(2,1)}, u32[]{:S(2)}) copy-start(bf16[256,256]{1,0:T(8,128)(2,1)} %constant.10.clone.m_z) | copy-start | bytes 393220
  13.0 0.9 %copy-start.7 = (bf16[256,256]{1,0:T(8,128)(2,1)S(1)}, bf16[256,256]{1,0:T(8,128)(2,1)}, u32[]{:S(2)}) copy-start(bf16[256,256]{1,0:T(8,128)(2,1)} %constant.9.clone.m_face) | copy-start | bytes 393220
  13.9 0.9 %copy-start.8 = (bf16[256,256]{1,0:T(8,128)(2,1)S(1)}, bf16[256,256]{1,0:T(8,128)(2,1)}, u32[]{:S(2)}) copy-start(bf16[256,256]{1,0:T(8,128)(2,1)} %constant.8.clone.m_in) | copy-start | bytes 393220
  14.8 0.8 %copy-start.9 = (bf16[128,256]{1,0:T(8,128)(2,1)S(1)}, bf16[128,256]{1,0:T(8,128)(2,1)}, u32[]{:S(2)}) copy-start(bf16[128,256]{1,0:T(8,128)(2,1)} %constant.11.clone.m_end) | copy-start | bytes 196612
where the time goes:
time: 43.2 us; the launch traced here: 43 us
  Pallas kernels  28.6 us (66%)
  local copies, waits for them, and re-layouts  7.45 us (17%)
  blocking collectives  6.2 us (14%)
  between operations  0.73 us (2%)
    pallas_call x1, Pallas kernels, wave(): pl.pallas_call(functools.partial(wave_kernel, sizes, ny), out_shape=[jax....  25.2 us
    unnamed x29, local copies, waits for them, and re-layouts  7.45 us
    all_gather x1, blocking collectives, shards(): gathered = lax.all_gather(residual, 'gz', axis=1, tiled=True)  6.2 us
    pallas_call x1, Pallas kernels, build_sources(): pl.pallas_call(functools.partial(source_kernel, block), out_shape=jax.Sha...  3.39 us

commit v1 on v0

v1 whole, which is shorter than its diff:
```python
import functools

import jax
import jax.numpy as jnp
import ml_dtypes
import numpy as np
from jax import lax
from jax.experimental import pallas as pl
from jax.experimental.pallas import tpu as pltpu
from jax.sharding import PartitionSpec as P

C = (-205.0 / 72.0, 8.0 / 5.0, -1.0 / 5.0, 8.0 / 315.0, -1.0 / 560.0)
AXES = ("gx", "gy", "gz")
MESH = pl.DeviceIdType.MESH


def split3(v):
    hi = v.astype(jnp.bfloat16)
    rest = v - hi.astype(jnp.float32)
    mid = rest.astype(jnp.bfloat16)
    lo = (rest - mid.astype(jnp.float32)).astype(jnp.bfloat16)
    return [hi, mid, lo]


def nt(a, b):
    return lax.dot_general(a, b, (((1,), (1,)), ((), ())), preferred_element_type=jnp.float32)


def source_kernel(block, res_ref, cell_ref, off_ref, w_ref, tr_ref, out_ref, table, info):
    bx, by, bz = block
    starts = [lax.axis_index(a) * n for a, n in zip(AXES, block)]
    taps, mics = w_ref.shape
    steps = res_ref.shape[1]
    rel = [cell_ref[d : d + 1, :] - starts[d] for d in range(3)]
    near = functools.reduce(
        jnp.logical_and, [(rel[d] >= -4) & (rel[d] < block[d] + 4) for d in range(3)]
    )
    at = [rel[d] + off_ref[d] for d in range(3)]
    inside = functools.reduce(
        jnp.logical_and, [(at[d] >= 0) & (at[d] < block[d]) for d in range(3)]
    )
    row = jnp.where(inside, at[0] * by + at[1], -1)
    col = jnp.where(inside, at[2], -1)
    table[0:taps, :] = row.astype(jnp.float32).astype(jnp.bfloat16)
    table[taps : 2 * taps, :] = col.astype(jnp.float32).astype(jnp.bfloat16)
    for i, part in enumerate(split3(w_ref[...])):
        table[(2 + i) * taps : (3 + i) * taps, :] = part
    near_f = jnp.where(near, 1.0, 0.0)
    lanes = 128
    blocks = mics // lanes
    tri = (
        lax.broadcasted_iota(jnp.int32, (lanes, lanes), 0)
        < lax.broadcasted_iota(jnp.int32, (lanes, lanes), 1)
    )
    tri = jnp.where(tri, 1.0, 0.0).astype(jnp.bfloat16)
    base = jnp.float32(0.0)
    for i in range(blocks):
        part = near_f[:, i * lanes : (i + 1) * lanes]
        before = jnp.dot(
            jnp.broadcast_to(part, (8, lanes)).astype(jnp.bfloat16),
            tri,
            preferred_element_type=jnp.float32,
        )[0:1]
        slot = jnp.where(part > 0.5, before + base, -1.0)
        info[0:1, i * lanes : (i + 1) * lanes] = slot
        base = base + jnp.sum(part)
    count = base.astype(jnp.int32)
    out_ref[...] = jnp.zeros_like(out_ref)
    share = 2
    held = lanes // share
    per = taps // share
    part_of = lax.broadcasted_iota(jnp.int32, (per, lanes), 1) // held

    def spread(v):
        out = v[0:per]
        for i in range(1, share):
            out = jnp.where(part_of == i, v[i * per : (i + 1) * per], out)
        return out

    def chunk(j, carry):
        slots = (lax.broadcasted_iota(jnp.int32, (lanes, mics), 0) % held + j * held).astype(jnp.float32)
        sel = jnp.where(slots == info[0:1, :], 1.0, 0.0)
        mic_id = lax.broadcasted_iota(jnp.int32, (1, mics), 1).astype(jnp.float32)
        mic = jnp.sum(sel * (mic_id + 1.0), axis=1, keepdims=True) - 1.0
        sel_r = jnp.where(tr_ref[...].astype(jnp.float32) == mic, 1.0, 0.0).astype(jnp.bfloat16)
        tab = nt(table[...], sel.astype(jnp.bfloat16))
        rows = spread(tab[0:taps])
        cols = spread(tab[taps : 2 * taps])
        weights = spread(
            tab[2 * taps : 3 * taps] + tab[3 * taps : 4 * taps] + tab[4 * taps : 5 * taps]
        )
        whole = jnp.concatenate([res_ref[g] for g in range(res_ref.shape[0])], axis=1)
        res = sum(nt(part, sel_r) for part in split3(whole))
        iota_row = lax.broadcasted_iota(jnp.int32, (bx * by, lanes), 0).astype(jnp.float32)
        iota_col = lax.broadcasted_iota(jnp.int32, (bz, lanes), 0).astype(jnp.float32)
        group = 4
        for t0 in range(0, per, group):
            left, right = [[] for _ in range(steps)], []
            for t in range(t0, t0 + group):
                row_hot = iota_row == rows[t : t + 1]
                col_hot = jnp.where(iota_col == cols[t : t + 1], 1.0, 0.0).astype(jnp.bfloat16)
                right += [col_hot, col_hot]
                for n in range(steps):
                    amount = weights[t : t + 1] * res[n : n + 1]
                    hi = amount.astype(jnp.bfloat16).astype(jnp.float32)
                    lo = amount - hi
                    left[n].append(jnp.where(row_hot, hi, 0.0).astype(jnp.bfloat16))
                    left[n].append(jnp.where(row_hot, lo, 0.0).astype(jnp.bfloat16))
            right = jnp.concatenate(right, axis=1)
            for n in range(steps):
                out_ref[n] += nt(jnp.concatenate(left[n], axis=1), right)
        return carry

    lax.fori_loop(0, (count + held - 1) // held, chunk, 0)


def build_sources(block, residual, receiver_cell, tap_offset, tap_weight, trace_receiver):
    steps = residual.shape[1]
    taps, mics = tap_weight.shape
    return pl.pallas_call(
        functools.partial(source_kernel, block),
        out_shape=jax.ShapeDtypeStruct((steps, block[0] * block[1], block[2]), jnp.float32),
        in_specs=[pl.BlockSpec(memory_space=pltpu.VMEM)] * 5,
        out_specs=pl.BlockSpec(memory_space=pltpu.VMEM),
        scratch_shapes=[
            pltpu.VMEM((5 * taps, mics), jnp.bfloat16),
            pltpu.VMEM((8, mics), jnp.float32),
        ],
        compiler_params=pltpu.CompilerParams(vmem_limit_bytes=40 * 2**20),
        name="sources",
    )(residual, receiver_cell, tap_offset, tap_weight, trace_receiver.reshape(1, mics))


def matrices(nx, ny, nz):
    weight = {k: round(5040 * C[abs(k)]) if k else 0 for k in range(-4, 5)}
    at = np.vectorize(lambda k: weight.get(int(k), 0))
    x, y = np.divmod(np.arange(nx * ny), ny)
    dx, dy = x[:, None] - x[None, :], y[:, None] - y[None, :]
    inner = at(dx) * (dy == 0) + at(dy) * (dx == 0)
    fx, fy = np.divmod(np.arange(4 * ny), ny)
    tile, sub = np.divmod(np.arange(4 * nx), 8)
    lo_x = tile + np.where(sub >= 4, 0, nx // 2)
    hi_x = tile + np.where(sub < 4, 0, nx // 2)
    face_x = np.concatenate([fx - 4, fx + nx, lo_x, hi_x])
    face_y = np.concatenate([fy, fy, sub % 4 - 4, sub % 4 + ny])
    dx, dy = x[:, None] - face_x[None, :], y[:, None] - face_y[None, :]
    faces = at(dx) * (dy == 0) + at(dy) * (dx == 0)
    z = np.arange(nz)
    along = at(z[:, None] - z[None, :])
    end = np.arange(128)
    end = np.where(end < 64, end + nz, end - 128)
    ends = at(end[:, None] - z[None, :])
    return [m.astype(ml_dtypes.bfloat16) for m in (inner, faces, along, ends)]


def nn(a, b):
    return jnp.dot(a, b, preferred_element_type=jnp.float32)


class Halo:
    def __init__(self, sizes, ny, shape, hl, zl, ys, send_sem, recv_sem):
        self.ny, (self.rows, self.nz) = ny, shape
        self.nx = self.rows // ny
        self.hl, self.zl, self.ys = hl, zl, ys
        self.send_sem, self.recv_sem = send_sem, recv_sem
        me = [lax.axis_index(a) for a in AXES]
        self.has, self.to = [], []
        for d in range(3):
            self.has += [me[d] > 0, me[d] < sizes[d] - 1]
            self.to += [
                {AXES[d]: jnp.maximum(me[d] - 1, 0)},
                {AXES[d]: jnp.minimum(me[d] + 1, sizes[d] - 1)},
            ]

    def landing(self, slot, f):
        edge = (4 * self.ny, 4 * self.ny, 4 * self.nx, 4 * self.nx)
        if f >= 4:
            return self.zl.at[slot, f - 4]
        return self.hl.at[slot, pl.ds(sum(edge[:f]), edge[f])]

    def copy(self, slot, f_ref, f):
        rows, face = self.rows, 4 * self.ny
        src = (
            f_ref.at[pl.ds(0, face)],
            f_ref.at[pl.ds(rows - face, face)],
            self.ys.at[slot, 0],
            self.ys.at[slot, 1],
            f_ref.at[pl.ds(0, rows), pl.ds(0, 128)],
            f_ref.at[pl.ds(0, rows), pl.ds(self.nz - 128, 128)],
        )[f]
        return pltpu.make_async_remote_copy(
            src_ref=src,
            dst_ref=self.landing(slot, f ^ 1),
            send_sem=self.send_sem.at[slot, f],
            recv_sem=self.recv_sem.at[slot, f ^ 1],
            device_id=self.to[f],
            device_id_type=MESH,
        )

    def send(self, slot, f_ref):
        sub = lax.broadcasted_iota(jnp.int32, (8, self.nz), 0)
        nx, ny, ys = self.nx, self.ny, self.ys

        def start(f):
            @pl.when(self.has[f])
            def _():
                self.copy(slot, f_ref, f).start()

        for f in (0, 1, 4, 5):
            start(f)
        for i in range(nx // 2):
            lo, far = i * ny, (i + nx // 2) * ny
            a, b = f_ref[lo : lo + 8], f_ref[far : far + 8]
            ys[slot, 0, 8 * i : 8 * i + 8] = jnp.where(sub < 4, a, pltpu.roll(b, 4, 0))
            a, b = f_ref[lo + ny - 8 : lo + ny], f_ref[far + ny - 8 : far + ny]
            ys[slot, 1, 8 * i : 8 * i + 8] = jnp.where(sub >= 4, a, pltpu.roll(b, 4, 0))
        for f in (2, 3):
            start(f)

    def land(self, slot, faces):
        for f in faces:
            @pl.when(self.has[f])
            def _(f=f):
                dst = self.landing(slot, f)
                pltpu.make_async_remote_copy(
                    src_ref=dst, dst_ref=dst,
                    send_sem=self.send_sem.at[slot, f], recv_sem=self.recv_sem.at[slot, f],
                    device_id=self.to[f], device_id_type=MESH,
                ).wait_recv()

    def clear(self, slots):
        for f in range(6):
            @pl.when(jnp.logical_not(self.has[f]))
            def _(f=f):
                for slot in range(slots):
                    dst = self.landing(slot, f)
                    dst[...] = jnp.zeros(dst.shape, jnp.float32)

    def drain(self, slot, f_ref):
        for f in range(6):
            @pl.when(self.has[f])
            def _(f=f):
                self.copy(slot, f_ref, f).wait_send()


def local(f_ref, out, mats):
    f = f_ref[...]
    acc = 0.0
    for part in split3(f):
        acc = acc + nn(mats[0][...], part) + nn(part, mats[2][...])
    out[...] = acc * (1.0 / 5040.0) + (3.0 * C[0]) * f


def finish(halo, slot, out, mats):
    halo.land(slot, range(6))
    acc = 0.0
    for part in split3(halo.hl[slot]):
        acc = acc + nn(mats[1][...], part)
    lane = lax.broadcasted_iota(jnp.int32, (halo.rows, 128), 1)
    for part in split3(jnp.where(lane < 64, halo.zl[slot, 1], halo.zl[slot, 0])):
        acc = acc + nn(part, mats[3][...])
    return out[...] + acc * (1.0 / 5040.0)


def load(mats_in, mats, sem):
    moves = [pltpu.make_async_copy(a, b, sem.at[i]) for i, (a, b) in enumerate(zip(mats_in, mats))]
    for move in moves:
        move.start()
    return moves


def greet(halo, extra=()):
    barrier = pltpu.get_barrier_semaphore()
    for f in range(4 if extra else 6):
        @pl.when(halo.has[f])
        def _(f=f):
            pl.semaphore_signal(barrier, inc=1, device_id=halo.to[f], device_id_type=MESH)
    for other in extra:
        pl.semaphore_signal(barrier, inc=1, device_id=other, device_id_type=MESH)
    count = sum(h.astype(jnp.int32) for h in halo.has[: 4 if extra else 6])
    pl.semaphore_wait(barrier, count + len(extra))


def first_kernel(
    sizes, ny, p0, p1, q5, q4, cf, res, *rest
):
    mats_in, (p2, p3, lap1, lap2, q3, res_all) = rest[:4], rest[4:10]
    mats, (fq, lq, gath, hl, zl, ys, send_sem, recv_sem, mat_sem, res_send, res_recv) = (
        rest[10:14], rest[14:],
    )
    moves = load(mats_in, mats, mat_sem)
    halo = Halo(sizes, ny, p0.shape, hl, zl, ys, send_sem, recv_sem)
    gz, n = lax.axis_index("gz"), sizes[2]
    ahead = [{"gz": lax.rem(gz + k, n)} for k in range(1, n)]
    greet(halo, ahead)

    res_moves = [
        pltpu.make_async_remote_copy(
            src_ref=res, dst_ref=gath.at[gz],
            send_sem=res_send.at[k], recv_sem=res_recv.at[k],
            device_id=ahead[k], device_id_type=MESH,
        )
        for k in range(n - 1)
    ]
    for move in res_moves:
        move.start()
    halo.send(0, p1)
    fq[...] = cf[...] * q4[...]
    halo.send(1, fq)
    gath[gz] = res[...]
    halo.clear(3)
    for move in moves:
        move.wait()
    local(p1, lap1, mats)
    local(fq, lq, mats)
    full = finish(halo, 0, lap1, mats)
    lap1[...] = full
    p2[...] = 2.0 * p1[...] - p0[...] + cf[...] * full
    halo.send(2, p2)
    local(p2, lap2, mats)
    q3[...] = 2.0 * q4[...] - q5[...] + finish(halo, 1, lq, mats)
    for k in range(n - 1):
        dst = gath.at[lax.rem(gz + n - 1 - k, n)]
        pltpu.make_async_remote_copy(
            src_ref=dst, dst_ref=dst,
            send_sem=res_send.at[k], recv_sem=res_recv.at[k],
            device_id=ahead[k], device_id_type=MESH,
        ).wait_recv()
    res_all[...] = gath[...]
    full = finish(halo, 2, lap2, mats)
    lap2[...] = full
    p3[...] = 2.0 * p2[...] - p1[...] + cf[...] * full
    halo.drain(0, p1)
    halo.drain(1, fq)
    halo.drain(2, p2)
    for move in res_moves:
        move.wait_send()


def last_kernel(sizes, ny, steps, q4, cf, q3_part, lap1, lap2, p2, p3, src, *rest):
    mats_in, (grad, one, zero) = rest[:4], rest[4:7]
    mats, (fp, fq, lap, lq, qb, hl, zl, ys, send_sem, recv_sem, mat_sem) = rest[7:11], rest[11:]
    moves = load(mats_in, mats, mat_sem)
    halo = Halo(sizes, ny, cf.shape, hl, zl, ys, send_sem, recv_sem)
    greet(halo)

    def p_at(n):
        return {2: p2, 3: p3}[n] if n < 4 else fp.at[n - 4]

    def lap_at(n):
        return {1: lap1, 2: lap2}[n] if n < 3 else lap.at[n - 3]

    forward = steps - 2
    qb[0] = q3_part[...] + src[steps - 1]
    fq[0] = cf[...] * qb[0]
    halo.send(forward, fq.at[0])
    halo.send(0, p3)
    halo.clear(forward + steps - 1)
    for move in moves:
        move.wait()
    local(fq.at[0], lq, mats)
    local(p3, lap.at[0], mats)
    for r in range(1, steps):
        slot = forward + r - 1
        full = finish(halo, slot, lq, mats)
        now = qb.at[r - 1]
        old = q4 if r == 1 else qb.at[r - 2]
        new = 2.0 * now[...] - old[...] + full + src[steps - 1 - r]
        if r + 1 < steps:
            qb[r] = new
            fq[r] = cf[...] * new
            halo.send(slot + 1, fq.at[r])
            local(fq.at[r], lq, mats)
        else:
            zero[...] = new
            one[...] = now[...]
        n = r + 2
        if n <= steps:
            full = finish(halo, n - 3, lap_at(n), mats)
            lap_at(n)[...] = full
            if n < steps:
                fp[n - 3] = 2.0 * p_at(n)[...] - p_at(n - 1)[...] + cf[...] * full
                halo.send(n - 2, fp.at[n - 3])
                local(fp.at[n - 3], lap_at(n + 1), mats)
        if r == steps - 2:
            total = q4[...] * lap_at(steps)[...]
            for m in range(1, steps):
                total = total + qb[m - 1] * lap_at(steps - m)[...]
            grad[...] = total
    for n in range(3, steps + 1):
        halo.drain(n - 3, p_at(n))
    for r in range(1, steps):
        halo.drain(forward + r - 1, fq.at[r - 1])


def shards(sizes, p0, p1, q5, q4, cf, residual, receiver_cell, tap_offset, tap_weight, trace_receiver):
    nx, ny, nz = p0.shape
    steps = residual.shape[0]
    rows = nx * ny
    f32 = jnp.float32
    vmem, anywhere = pl.BlockSpec(memory_space=pltpu.VMEM), pl.BlockSpec(memory_space=pl.ANY)
    p0, p1, q5, q4, cf = [a.reshape(rows, nz) for a in (p0, p1, q5, q4, cf)]
    mats = matrices(nx, ny, nz)
    field = jax.ShapeDtypeStruct((rows, nz), f32)
    mat_scratch = [pltpu.VMEM(m.shape, jnp.bfloat16) for m in mats]

    def halo_scratch(slots):
        return [
            pltpu.VMEM((slots, 8 * (nx + ny), nz), f32),
            pltpu.VMEM((slots, 2, rows, 128), f32),
            pltpu.VMEM((slots, 2, 4 * nx, nz), f32),
            pltpu.SemaphoreType.DMA((slots, 6)),
            pltpu.SemaphoreType.DMA((slots, 6)),
            pltpu.SemaphoreType.DMA((4,)),
        ]

    gath = (sizes[2],) + residual.shape
    p2, p3, lap1, lap2, q3, res_all = pl.pallas_call(
        functools.partial(first_kernel, sizes, ny),
        out_shape=[field] * 5 + [jax.ShapeDtypeStruct(gath, f32)],
        in_specs=[vmem] * 6 + [anywhere] * 4,
        out_specs=[vmem] * 6,
        scratch_shapes=mat_scratch
        + [pltpu.VMEM((rows, nz), f32), pltpu.VMEM((rows, nz), f32), pltpu.VMEM(gath, f32)]
        + halo_scratch(3)
        + [pltpu.SemaphoreType.DMA((sizes[2],)), pltpu.SemaphoreType.DMA((sizes[2],))],
        compiler_params=pltpu.CompilerParams(
            collective_id=0, has_side_effects=True, vmem_limit_bytes=28 * 2**20
        ),
        name="first",
    )(p0, p1, q5, q4, cf, residual, *mats)
    src = build_sources((nx, ny, nz), res_all, receiver_cell, tap_offset, tap_weight, trace_receiver)
    outs = pl.pallas_call(
        functools.partial(last_kernel, sizes, ny, steps),
        out_shape=[field] * 3,
        in_specs=[vmem] * 8 + [anywhere] * 4,
        out_specs=[vmem] * 3,
        scratch_shapes=mat_scratch
        + [
            pltpu.VMEM((steps - 3, rows, nz), f32),
            pltpu.VMEM((steps - 1, rows, nz), f32),
            pltpu.VMEM((steps - 2, rows, nz), f32),
            pltpu.VMEM((rows, nz), f32),
            pltpu.VMEM((steps - 1, rows, nz), f32),
        ]
        + halo_scratch(2 * steps - 3),
        compiler_params=pltpu.CompilerParams(
            collective_id=1, has_side_effects=True, vmem_limit_bytes=40 * 2**20
        ),
        name="last",
    )(q4, cf, q3, lap1, lap2, p2, p3, src, *mats)
    return tuple(o.reshape(nx, ny, nz) for o in outs)


def solution(mesh):
    field = P(*AXES)
    return jax.shard_map(
        functools.partial(shards, tuple(mesh.shape[a] for a in AXES)),
        mesh=mesh,
        in_specs=(field,) * 5 + (P(None, "gz"), P(), P(), P(), P()),
        out_specs=(field,) * 3,
        check_vma=False,
    )
```

time: 43.2 us -> 46.6 us (1.079); the launches traced: 43 us -> 45.7 us
  blocking collectives: 6.2 us -> 0 us
  Pallas kernels: 28.6 us -> 33.2 us
  local copies, waits for them, and re-layouts: 7.45 us -> 11.8 us
    all_gather x1 -> x0, blocking collectives: 6.2 us -> none  [shards(): gathered = lax.all_gather(residual, 'gz', axis=1, tiled=True)]
    pallas_call x1 -> x2, Pallas kernels: 25.2 us -> 30.9 us  [the longest x1 17.4 us: shards(): pl.pallas_call(functools.partial(last_kernel, sizes, ny, steps), out_shap...]
    unnamed x29 -> x43, local copies, waits for them, and re-layouts: 7.45 us -> 11.8 us
    pallas_call x1, Pallas kernels: 3.39 us -> 2.3 us  [build_sources(): pl.pallas_call(functools.partial(source_kernel, block), out_shape=jax.Sha...]
where the time goes in v1:
time: 46.6 us; the launch traced here: 45.7 us
  Pallas kernels  33.2 us (71%)
  local copies, waits for them, and re-layouts  11.8 us (25%)
  between operations  0.78 us (2%)
    pallas_call x1, Pallas kernels, shards(): pl.pallas_call(functools.partial(last_kernel, sizes, ny, steps), out_shap...  17.4 us
    pallas_call x1, Pallas kernels, shards(): pl.pallas_call(functools.partial(first_kernel, sizes, ny), out_shape=[fie...  13.4 us
    unnamed x43, local copies, waits for them, and re-layouts  11.8 us
    pallas_call x1, Pallas kernels, build_sources(): pl.pallas_call(functools.partial(source_kernel, block), out_shape=jax.Sha...  2.3 us

profile of v1, /device:TPU:1, one launch (start us, length us, event | category | flops | bytes accessed | tf_op | source)
XLA Modules:
  0.0 45.7 jit_solution(894149259787273516)
XLA Ops:
  0.6 0.0 copy-start.18
  0.6 0.7 %copy-done.18 = f32[4,256]{1,0:T(4,128)S(1)} copy-done((f32[4,256]{1,0:T(4,128)S(1)}, f32[4,256]{1,0:T(4,128)}, u32[]{:S(2)}) %copy-start.18) | copy-done | bytes 4120
  1.3 0.0 copy-start
  1.3 0.9 %copy-done = f32[16,16,256]{2,1,0:T(8,128)S(1)} copy-done((f32[16,16,256]{2,1,0:T(8,128)S(1)}, f32[16,16,256]{2,1,0:T(8,128)}, u32[]{:S(2)}) %copy-start) | copy-done | bytes 262168
  2.3 0.0 copy-start.2
  2.3 0.9 %copy-done.2 = f32[16,16,256]{2,1,0:T(8,128)S(1)} copy-done((f32[16,16,256]{2,1,0:T(8,128)S(1)}, f32[16,16,256]{2,1,0:T(8,128)}, u32[]{:S(2)}) %copy-start.2) | copy-done | bytes 262168
  3.2 0.0 copy-start.4
  3.2 0.9 %copy-done.4 = bf16[256,256]{1,0:T(8,128)(2,1)S(1)} copy-done((bf16[256,256]{1,0:T(8,128)(2,1)S(1)}, bf16[256,256]{1,0:T(8,128)(2,1)}, u32[]{:S(2)}) %copy-start.4) | copy-done | bytes 131096
  4.1 0.0 copy-start.6
  4.1 0.9 %copy-done.6 = bf16[256,256]{1,0:T(8,128)(2,1)S(1)} copy-done((bf16[256,256]{1,0:T(8,128)(2,1)S(1)}, bf16[256,256]{1,0:T(8,128)(2,1)}, u32[]{:S(2)}) %copy-start.6) | copy-done | bytes 131096
  5.0 0.0 copy-start.8
  5.0 0.9 %copy-done.8 = bf16[256,256]{1,0:T(8,128)(2,1)S(1)} copy-done((bf16[256,256]{1,0:T(8,128)(2,1)S(1)}, bf16[256,256]{1,0:T(8,128)(2,1)}, u32[]{:S(2)}) %copy-start.8) | copy-done | bytes 131096
  5.9 0.0 copy-start.10
  5.9 0.8 %copy-done.10 = bf16[128,256]{1,0:T(8,128)(2,1)S(1)} copy-done((bf16[128,256]{1,0:T(8,128)(2,1)S(1)}, bf16[128,256]{1,0:T(8,128)(2,1)}, u32[]{:S(2)}) %copy-start.10) | copy-done | bytes 65560
  6.8 0.0 copy-start.12
  6.8 0.9 %copy-done.12 = f32[16,16,256]{2,1,0:T(8,128)S(1)} copy-done((f32[16,16,256]{2,1,0:T(8,128)S(1)}, f32[16,16,256]{2,1,0:T(8,128)}, u32[]{:S(2)}) %copy-start.12) | copy-done | bytes 262168
  7.7 0.0 copy-start.13
  7.7 0.9 %copy-done.13 = f32[16,16,256]{2,1,0:T(8,128)S(1)} copy-done((f32[16,16,256]{2,1,0:T(8,128)S(1)}, f32[16,16,256]{2,1,0:T(8,128)}, u32[]{:S(2)}) %copy-start.13) | copy-done | bytes 262168
  8.7 0.0 copy-start.14
  8.7 0.9 %copy-done.14 = f32[16,16,256]{2,1,0:T(8,128)S(1)} copy-done((f32[16,16,256]{2,1,0:T(8,128)S(1)}, f32[16,16,256]{2,1,0:T(8,128)}, u32[]{:S(2)}) %copy-start.14) | copy-done | bytes 262168
  9.6 0.0 copy-start.15
  9.6 0.0 copy-start.16
  9.6 0.0 copy-start.17
  9.6 13.4 %first.1 = (f32[256,256]{1,0:T(8,128)S(1)}, f32[256,256]{1,0:T(8,128)S(1)}, f32[256,256]{1,0:T(8,128)S(1)}, f32[256,256]{1,0:T(8,128)S(1)}, f32[256,256]{1,0:T(8,128)S(1)}, /*index=5*/f32[4,4,256]{2,1,0:T(4,128)S(1)}) custom-call(f32[256,256]{1,0:T(8,128)S(1)} %bitcast.13, f32[256,256]{1,0:T(8,128)S(1)} %bitcast.14, f32[256,256]{1,0:T(8,128)S(1)} %bitcast.15, ...), custom_call_target="tpu_custom_call" | custom-call | tf_op jit(solution)/shard_map/first/pallas_call | solution.py:418
  23.1 0.0 copy-start.19
  23.1 0.0 copy-done.15
  23.1 0.0 copy-done.16
  23.1 0.0 copy-done.17
  23.1 0.6 %copy-done.19 = s32[1024]{0:T(1024)S(1)} copy-done((s32[1024]{0:T(1024)S(1)}, s32[1024]{0:T(1024)}, u32[]{:S(2)}) %copy-start.19) | copy-done | bytes 4120
  23.7 0.0 copy-start.1
  23.7 0.0 copy-start.3
  23.7 0.0 copy-start.5
  23.8 0.0 copy-start.7
  23.8 0.0 copy-start.9
  23.8 0.0 copy-start.11
  23.8 2.3 %sources.1.src = f32[4,256,256]{2,1,0:T(8,128)S(1)} custom-call(f32[4,4,256]{2,1,0:T(4,128)S(1)} %get-tuple-element.17.res_ref, s32[3,1024]{1,0:T(4,128)S(1)} %copy-done.17, s32[3,16,1024]{2,1,0:T(8,128)S(1)} %copy-done.15, f32[16,1024]{1,0:T(8,128)S(1)} %copy-done.16, s32[1,1024]{1,0:T(1,128)S(1)} %bitcast.19), custom_call_target="tpu_custom_call" | custom-call | tf_op jit(solution)/shard_map/sources/pallas_call | solution.py:120
  26.1 0.0 copy-done.1
  26.1 0.0 copy-done.3
  26.1 0.0 copy-done.5
  26.1 0.0 copy-done.7
  26.1 0.0 copy-done.9
  26.1 0.0 copy-done.11
  26.1 17.4 %last.1 = (f32[256,256]{1,0:T(8,128)S(1)}, f32[256,256]{1,0:T(8,128)S(1)}, f32[256,256]{1,0:T(8,128)S(1)}) custom-call(f32[256,256]{1,0:T(8,128)S(1)} %bitcast.10, f32[256,256]{1,0:T(8,128)S(1)} %bitcast.12, f32[256,256]{1,0:T(8,128)S(1)} %get-tuple-element.12.q3_part, f32[256,256]{1,0:T(8,128)S(1)} %get-tuple-element.13.lap1, ...), custom_call_target="tpu_custom_call" | custom-call | tf_op jit(solution)/shard_map/last/pallas_call | solution.py:433
  43.6 0.7 %copy.20 = f32[16,16,256]{2,1,0:T(8,128)} copy(f32[16,16,256]{2,1,0:T(8,128)S(1)} %bitcast.18) | data formatting | bytes 524288
  44.3 0.7 %copy.21 = f32[16,16,256]{2,1,0:T(8,128)} copy(f32[16,16,256]{2,1,0:T(8,128)S(1)} %bitcast.17) | data formatting | bytes 524288
  45.0 0.7 %copy.22 = f32[16,16,256]{2,1,0:T(8,128)} copy(f32[16,16,256]{2,1,0:T(8,128)S(1)} %bitcast.16) | data formatting | bytes 524288
Async XLA Ops:
  0.6 0.7 %copy-start.18 = (f32[4,256]{1,0:T(4,128)S(1)}, f32[4,256]{1,0:T(4,128)}, u32[]{:S(2)}) copy-start(f32[4,256]{1,0:T(4,128)} %res.1) | copy-start | bytes 12292
  1.3 0.9 %copy-start = (f32[16,16,256]{2,1,0:T(8,128)S(1)}, f32[16,16,256]{2,1,0:T(8,128)}, u32[]{:S(2)}) copy-start(f32[16,16,256]{2,1,0:T(8,128)} %param.17) | copy-start | bytes 786436
  2.3 0.9 %copy-start.2 = (f32[16,16,256]{2,1,0:T(8,128)S(1)}, f32[16,16,256]{2,1,0:T(8,128)}, u32[]{:S(2)}) copy-start(f32[16,16,256]{2,1,0:T(8,128)} %param.18) | copy-start | bytes 786436
  3.2 0.9 %copy-start.4 = (bf16[256,256]{1,0:T(8,128)(2,1)S(1)}, bf16[256,256]{1,0:T(8,128)(2,1)}, u32[]{:S(2)}) copy-start(bf16[256,256]{1,0:T(8,128)(2,1)} %constant.10.clone.rest_2_) | copy-start | bytes 393220
  4.1 0.9 %copy-start.6 = (bf16[256,256]{1,0:T(8,128)(2,1)S(1)}, bf16[256,256]{1,0:T(8,128)(2,1)}, u32[]{:S(2)}) copy-start(bf16[256,256]{1,0:T(8,128)(2,1)} %constant.9.clone.rest_1_) | copy-start | bytes 393220
  5.0 0.9 %copy-start.8 = (bf16[256,256]{1,0:T(8,128)(2,1)S(1)}, bf16[256,256]{1,0:T(8,128)(2,1)}, u32[]{:S(2)}) copy-start(bf16[256,256]{1,0:T(8,128)(2,1)} %constant.8.clone.rest_0_) | copy-start | bytes 393220
  5.9 0.8 %copy-start.10 = (bf16[128,256]{1,0:T(8,128)(2,1)S(1)}, bf16[128,256]{1,0:T(8,128)(2,1)}, u32[]{:S(2)}) copy-start(bf16[128,256]{1,0:T(8,128)(2,1)} %constant.11.clone.rest_3_) | copy-start | bytes 196612
  6.8 0.9 %copy-start.12 = (f32[16,16,256]{2,1,0:T(8,128)S(1)}, f32[16,16,256]{2,1,0:T(8,128)}, u32[]{:S(2)}) copy-start(f32[16,16,256]{2,1,0:T(8,128)} %param.14) | copy-start | bytes 786436
  7.7 0.9 %copy-start.13 = (f32[16,16,256]{2,1,0:T(8,128)S(1)}, f32[16,16,256]{2,1,0:T(8,128)}, u32[]{:S(2)}) copy-start(f32[16,16,256]{2,1,0:T(8,128)} %param.15) | copy-start | bytes 786436
  8.7 0.9 %copy-start.14 = (f32[16,16,256]{2,1,0:T(8,128)S(1)}, f32[16,16,256]{2,1,0:T(8,128)}, u32[]{:S(2)}) copy-start(f32[16,16,256]{2,1,0:T(8,128)} %param.16) | copy-start | bytes 786436
  9.6 13.4 %copy-start.15 = (s32[3,16,1024]{2,1,0:T(8,128)S(1)}, s32[3,16,1024]{2,1,0:T(8,128)}, u32[]{:S(2)}) copy-start(s32[3,16,1024]{2,1,0:T(8,128)} %off_ref.1) | copy-start | bytes 589828
  9.6 13.4 %copy-start.16 = (f32[16,1024]{1,0:T(8,128)S(1)}, f32[16,1024]{1,0:T(8,128)}, u32[]{:S(2)}) copy-start(f32[16,1024]{1,0:T(8,128)} %w_ref.1) | copy-start | bytes 196612
  9.6 13.5 %copy-start.17 = (s32[3,1024]{1,0:T(4,128)S(1)}, s32[3,1024]{1,0:T(4,128)}, u32[]{:S(2)}) copy-start(s32[3,1024]{1,0:T(4,128)} %cell_ref.1) | copy-start | bytes 36868
  23.1 0.7 %copy-start.19 = (s32[1024]{0:T(1024)S(1)}, s32[1024]{0:T(1024)}, u32[]{:S(2)}) copy-start(s32[1024]{0:T(1024)} %param.23) | copy-start | bytes 12292
  23.7 2.3 %copy-start.1 = (f32[16,16,256]{2,1,0:T(8,128)S(1)}, f32[16,16,256]{2,1,0:T(8,128)}, u32[]{:S(2)}) copy-start(f32[16,16,256]{2,1,0:T(8,128)} %param.17) | copy-start | bytes 786436
  23.7 2.4 %copy-start.3 = (f32[16,16,256]{2,1,0:T(8,128)S(1)}, f32[16,16,256]{2,1,0:T(8,128)}, u32[]{:S(2)}) copy-start(f32[16,16,256]{2,1,0:T(8,128)} %param.18) | copy-start | bytes 786436
  23.7 2.4 %copy-start.5 = (bf16[256,256]{1,0:T(8,128)(2,1)S(1)}, bf16[256,256]{1,0:T(8,128)(2,1)}, u32[]{:S(2)}) copy-start(bf16[256,256]{1,0:T(8,128)(2,1)} %constant.10.clone.rest_2_) | copy-start | bytes 393220
  23.8 2.4 %copy-start.7 = (bf16[256,256]{1,0:T(8,128)(2,1)S(1)}, bf16[256,256]{1,0:T(8,128)(2,1)}, u32[]{:S(2)}) copy-start(bf16[256,256]{1,0:T(8,128)(2,1)} %constant.9.clone.rest_1_) | copy-start | bytes 393220
  23.8 2.4 %copy-start.9 = (bf16[256,256]{1,0:T(8,128)(2,1)S(1)}, bf16[256,256]{1,0:T(8,128)(2,1)}, u32[]{:S(2)}) copy-start(bf16[256,256]{1,0:T(8,128)(2,1)} %constant.8.clone.rest_0_) | copy-start | bytes 393220
  23.8 2.4 %copy-start.11 = (bf16[128,256]{1,0:T(8,128)(2,1)S(1)}, bf16[128,256]{1,0:T(8,128)(2,1)}, u32[]{:S(2)}) copy-start(bf16[128,256]{1,0:T(8,128)(2,1)} %constant.11.clone.rest_3_) | copy-start | bytes 196612

commit v2 on v0

--- a/solution.py
+++ b/solution.py
@@ -2,8 +2,6 @@
 
 import jax
 import jax.numpy as jnp
-import ml_dtypes
-import numpy as np
 from jax import lax
 from jax.experimental import pallas as pl
 from jax.experimental.pallas import tpu as pltpu
@@ -30,7 +28,7 @@
     bx, by, bz = block
     starts = [lax.axis_index(a) * n for a, n in zip(AXES, block)]
     taps, mics = w_ref.shape
-    steps = res_ref.shape[0]
+    steps = res_ref.shape[1]
     rel = [cell_ref[d : d + 1, :] - starts[d] for d in range(3)]
     near = functools.reduce(
         jnp.logical_and, [(rel[d] >= -4) & (rel[d] < block[d] + 4) for d in range(3)]
@@ -66,22 +64,35 @@
         base = base + jnp.sum(part)
     count = base.astype(jnp.int32)
     out_ref[...] = jnp.zeros_like(out_ref)
+    share = 2
+    held = lanes // share
+    per = taps // share
+    part_of = lax.broadcasted_iota(jnp.int32, (per, lanes), 1) // held
+
+    def spread(v):
+        out = v[0:per]
+        for i in range(1, share):
+            out = jnp.where(part_of == i, v[i * per : (i + 1) * per], out)
+        return out
 
     def chunk(j, carry):
-        slots = (lax.broadcasted_iota(jnp.int32, (lanes, mics), 0) + j * lanes).astype(jnp.float32)
+        slots = (lax.broadcasted_iota(jnp.int32, (lanes, mics), 0) % held + j * held).astype(jnp.float32)
         sel = jnp.where(slots == info[0:1, :], 1.0, 0.0)
         mic_id = lax.broadcasted_iota(jnp.int32, (1, mics), 1).astype(jnp.float32)
         mic = jnp.sum(sel * (mic_id + 1.0), axis=1, keepdims=True) - 1.0
         sel_r = jnp.where(tr_ref[...].astype(jnp.float32) == mic, 1.0, 0.0).astype(jnp.bfloat16)
         tab = nt(table[...], sel.astype(jnp.bfloat16))
-        rows = tab[0:taps]
-        cols = tab[taps : 2 * taps]
-        weights = tab[2 * taps : 3 * taps] + tab[3 * taps : 4 * taps] + tab[4 * taps : 5 * taps]
-        res = sum(nt(part, sel_r) for part in split3(res_ref[...]))
+        rows = spread(tab[0:taps])
+        cols = spread(tab[taps : 2 * taps])
+        weights = spread(
+            tab[2 * taps : 3 * taps] + tab[3 * taps : 4 * taps] + tab[4 * taps : 5 * taps]
+        )
+        whole = jnp.concatenate([res_ref[g] for g in range(res_ref.shape[0])], axis=1)
+        res = sum(nt(part, sel_r) for part in split3(whole))
         iota_row = lax.broadcasted_iota(jnp.int32, (bx * by, lanes), 0).astype(jnp.float32)
         iota_col = lax.broadcasted_iota(jnp.int32, (bz, lanes), 0).astype(jnp.float32)
         group = 4
-        for t0 in range(0, taps, group):
+        for t0 in range(0, per, group):
             left, right = [[] for _ in range(steps)], []
             for t in range(t0, t0 + group):
                 row_hot = iota_row == rows[t : t + 1]
@@ -98,11 +109,11 @@
                 out_ref[n] += nt(jnp.concatenate(left[n], axis=1), right)
         return carry
 
-    lax.fori_loop(0, (count + lanes - 1) // lanes, chunk, 0)
+    lax.fori_loop(0, (count + held - 1) // held, chunk, 0)
 
 
 def build_sources(block, residual, receiver_cell, tap_offset, tap_weight, trace_receiver):
-    steps = residual.shape[0]
+    steps = residual.shape[1]
     taps, mics = tap_weight.shape
     return pl.pallas_call(
         functools.partial(source_kernel, block),
@@ -113,31 +124,98 @@
             pltpu.VMEM((5 * taps, mics), jnp.bfloat16),
             pltpu.VMEM((8, mics), jnp.float32),
         ],
-        compiler_params=pltpu.CompilerParams(vmem_limit_bytes=40 * 2**20),
+        compiler_params=pltpu.CompilerParams(vmem_limit_bytes=32 * 2**20),
         name="sources",
     )(residual, receiver_cell, tap_offset, tap_weight, trace_receiver.reshape(1, mics))
 
 
-def matrices(nx, ny, nz):
-    weight = {k: round(5040 * C[abs(k)]) if k else 0 for k in range(-4, 5)}
-    at = np.vectorize(lambda k: weight.get(int(k), 0))
-    x, y = np.divmod(np.arange(nx * ny), ny)
-    dx, dy = x[:, None] - x[None, :], y[:, None] - y[None, :]
-    inner = at(dx) * (dy == 0) + at(dy) * (dx == 0)
-    fx, fy = np.divmod(np.arange(4 * ny), ny)
-    tile, sub = np.divmod(np.arange(4 * nx), 8)
-    lo_x = tile + np.where(sub >= 4, 0, nx // 2)
-    hi_x = tile + np.where(sub < 4, 0, nx // 2)
-    face_x = np.concatenate([fx - 4, fx + nx, lo_x, hi_x])
-    face_y = np.concatenate([fy, fy, sub % 4 - 4, sub % 4 + ny])
-    dx, dy = x[:, None] - face_x[None, :], y[:, None] - face_y[None, :]
-    faces = at(dx) * (dy == 0) + at(dy) * (dx == 0)
-    z = np.arange(nz)
-    along = at(z[:, None] - z[None, :])
-    end = np.arange(128)
-    end = np.where(end < 64, end + nz, end - 128)
-    ends = at(end[:, None] - z[None, :])
-    return [m.astype(ml_dtypes.bfloat16) for m in (inner, faces, along, ends)]
+def stencil(d):
+    d = jnp.abs(d)
+    return sum(jnp.where(d == k, float(round(5040 * C[k])), 0.0) for k in range(1, 5))
+
+
+def cross(dx, dy):
+    return jnp.where(dy == 0, stencil(dx), 0.0) + jnp.where(dx == 0, stencil(dy), 0.0)
+
+
+def matrices(nx, ny, m_in, m_face, m_z, m_end):
+    def grid(ref):
+        return [lax.broadcasted_iota(jnp.int32, ref.shape, d) for d in range(2)]
+
+    to, at = grid(m_in)
+    m_in[...] = cross(to // ny - at // ny, to % ny - at % ny).astype(jnp.bfloat16)
+    to, at = grid(m_face)
+    x, y = to // ny, to % ny
+    upper = at >= 4 * ny
+    face = at - jnp.where(upper, 4 * ny, 0)
+    in_x = cross(x - (face // ny + jnp.where(upper, nx, -4)), y - face % ny)
+    pack = at - 8 * ny
+    upper = pack >= 4 * nx
+    pack = pack - jnp.where(upper, 4 * nx, 0)
+    far = jnp.where(pack % 8 < 4, 0, 1) == jnp.where(upper, 1, 0)
+    face_x = pack // 8 + jnp.where(far, nx // 2, 0)
+    in_y = cross(x - face_x, y - (pack % 4 + jnp.where(upper, ny, -4)))
+    m_face[...] = jnp.where(at < 8 * ny, in_x, in_y).astype(jnp.bfloat16)
+    at, to = grid(m_z)
+    m_z[...] = stencil(to - at).astype(jnp.bfloat16)
+    at, to = grid(m_end)
+    m_end[...] = stencil(to - jnp.where(at < 64, at + m_z.shape[0], at - 128)).astype(jnp.bfloat16)
+
+
+def gather_kernel(n, block, res, out, m_in, m_face, m_z, m_end, land, send_sem, recv_sem):
+    gz = lax.axis_index("gz")
+    ahead = [{"gz": lax.rem(gz + k, n)} for k in range(1, n)]
+    barrier = pltpu.get_barrier_semaphore()
+    for other in ahead:
+        pl.semaphore_signal(barrier, inc=1, device_id=other, device_id_type=MESH)
+    pl.semaphore_wait(barrier, n - 1)
+    moves = [
+        pltpu.make_async_remote_copy(
+            src_ref=res, dst_ref=land.at[gz],
+            send_sem=send_sem.at[k], recv_sem=recv_sem.at[k],
+            device_id=ahead[k], device_id_type=MESH,
+        )
+        for k in range(n - 1)
+    ]
+    for move in moves:
+        move.start()
+    matrices(block[0], block[1], m_in, m_face, m_z, m_end)
+    land[gz] = res[...]
+    for k in range(n - 1):
+        dst = land.at[lax.rem(gz + n - 1 - k, n)]
+        pltpu.make_async_remote_copy(
+            src_ref=dst, dst_ref=dst,
+            send_sem=send_sem.at[k], recv_sem=recv_sem.at[k],
+            device_id=ahead[k], device_id_type=MESH,
+        ).wait_recv()
+    out[...] = land[...]
+    for move in moves:
+        move.wait_send()
+
+
+def gather(sizes, block, residual):
+    nx, ny, nz = block
+    n = sizes[2]
+    vmem = pl.BlockSpec(memory_space=pltpu.VMEM)
+    shape = (n,) + residual.shape
+    mats = [(nx * ny, nx * ny), (nx * ny, 8 * (nx + ny)), (nz, nz), (128, nz)]
+    return pl.pallas_call(
+        functools.partial(gather_kernel, n, block),
+        out_shape=[jax.ShapeDtypeStruct(shape, jnp.float32)]
+        + [jax.ShapeDtypeStruct(m, jnp.bfloat16) for m in mats],
+        in_specs=[vmem],
+        out_specs=[vmem] * 5,
+        scratch_shapes=[
+            pltpu.VMEM(shape, jnp.float32),
+            pltpu.SemaphoreType.DMA((n,)),
+            pltpu.SemaphoreType.DMA((n,)),
+        ],
+        compiler_params=pltpu.CompilerParams(
+            collective_id=1, has_side_effects=True, vmem_limit_bytes=16 * 2**20
+        ),
+        cost_estimate=pl.CostEstimate(flops=4 * 10**9, bytes_accessed=12 * 10**6, transcendentals=0),
+        name="gather",
+    )(residual)
 
 
 def nn(a, b):
@@ -295,7 +373,7 @@
                     moves[f].wait_send()
 
 
-def wave(sizes, p0, p1, q5, q4, cf, src):
+def wave(sizes, p0, p1, q5, q4, cf, src, mats):
     nx, ny, nz = p0.shape
     steps = src.shape[0]
     rows = nx * ny
@@ -319,17 +397,17 @@
             pltpu.SemaphoreType.DMA((2, steps, 6)),
         ],
         compiler_params=pltpu.CompilerParams(
-            collective_id=0, has_side_effects=True, vmem_limit_bytes=48 * 2**20
+            collective_id=0, has_side_effects=True, vmem_limit_bytes=32 * 2**20
         ),
         name="wave",
-    )(*flat, src, *matrices(nx, ny, nz))
+    )(*flat, src, *mats)
     return [o.reshape(nx, ny, nz) for o in outs]
 
 
 def shards(sizes, p0, p1, q5, q4, cf, residual, receiver_cell, tap_offset, tap_weight, trace_receiver):
-    gathered = lax.all_gather(residual, "gz", axis=1, tiled=True)
+    gathered, *mats = gather(sizes, p0.shape, residual)
     src = build_sources(p0.shape, gathered, receiver_cell, tap_offset, tap_weight, trace_receiver)
-    return tuple(wave(sizes, p0, p1, q5, q4, cf, src))
+    return tuple(wave(sizes, p0, p1, q5, q4, cf, src, mats))
 
 
 def solution(mesh):

time: 43.2 us -> 36.8 us (0.85)
  the two profiles are of different devices: /device:TPU:1 before, /device:TPU:0 now
where the time goes in v2:
time: 36.8 us; the launch traced here: 36.7 us
  Pallas kernels  32.5 us (88%)
  local copies, waits for them, and re-layouts  3.47 us (9%)
  between operations  0.75 us (2%)
    pallas_call x1, Pallas kernels, wave(): pl.pallas_call(functools.partial(wave_kernel, sizes, ny), out_shape=[jax....  25.5 us
    pallas_call x1, Pallas kernels, gather(): pl.pallas_call(functools.partial(gather_kernel, n, block), out_shape=[jax...  4.64 us
    unnamed x23, local copies, waits for them, and re-layouts  3.47 us
    pallas_call x1, Pallas kernels, build_sources(): pl.pallas_call(functools.partial(source_kernel, block), out_shape=jax.Sha...  2.3 us

profile of v2, /device:TPU:0, one launch (start us, length us, event | category | flops | bytes accessed | tf_op | source)
XLA Modules:
  0.0 36.7 jit_solution(11558464661840860149)
XLA Ops:
  0.6 0.0 copy-start.9
  0.6 0.7 %copy-done.9 = f32[4,256]{1,0:T(4,128)S(1)} copy-done((f32[4,256]{1,0:T(4,128)S(1)}, f32[4,256]{1,0:T(4,128)}, u32[]{:S(2)}) %copy-start.9) | copy-done | bytes 4120
  1.3 0.0 copy-start.5
  1.3 0.0 copy-start.6
  1.3 0.0 copy-start.7
  1.3 4.6 %gather.1 = (f32[4,4,256]{2,1,0:T(4,128)S(1)}, bf16[256,256]{1,0:T(8,128)(2,1)S(1)}, bf16[256,256]{1,0:T(8,128)(2,1)S(1)}, bf16[256,256]{1,0:T(8,128)(2,1)S(1)}, bf16[128,256]{1,0:T(8,128)(2,1)S(1)}) custom-call(f32[4,256]{1,0:T(4,128)S(1)} %copy-done.9), custom_call_target="tpu_custom_call" | custom-call | flops 4000000000 | bytes 12000000 | tf_op jit(solution)/shard_map/gather/pallas_call | solution.py:202
  6.0 0.0 copy-start.8
  6.0 0.0 copy-done.5
  6.0 0.0 copy-done.6
  6.0 0.0 copy-done.7
  6.0 0.6 %copy-done.8 = s32[1024]{0:T(1024)S(1)} copy-done((s32[1024]{0:T(1024)S(1)}, s32[1024]{0:T(1024)}, u32[]{:S(2)}) %copy-start.8) | copy-done | bytes 4120
  6.7 0.0 copy-start
  6.7 0.0 copy-start.1
  6.7 0.0 copy-start.2
  6.7 0.0 copy-start.3
  6.7 0.0 copy-start.4
  6.7 2.3 %sources.1.src = f32[4,256,256]{2,1,0:T(8,128)S(1)} custom-call(f32[4,4,256]{2,1,0:T(4,128)S(1)} %get-tuple-element.11.res_ref, s32[3,1024]{1,0:T(4,128)S(1)} %copy-done.7, s32[3,16,1024]{2,1,0:T(8,128)S(1)} %copy-done.5, f32[16,1024]{1,0:T(8,128)S(1)} %copy-done.6, s32[1,1024]{1,0:T(1,128)S(1)} %bitcast.17), custom_call_target="tpu_custom_call" | custom-call | tf_op jit(solution)/shard_map/sources/pallas_call | solution.py:118
  9.0 0.0 copy-done
  9.0 0.0 copy-done.1
  9.0 0.0 copy-done.2
  9.0 0.0 copy-done.3
  9.0 0.0 copy-done.4
  9.1 25.5 %wave.1 = (f32[256,256]{1,0:T(8,128)S(1)}, f32[256,256]{1,0:T(8,128)S(1)}, f32[256,256]{1,0:T(8,128)S(1)}) custom-call(f32[256,256]{1,0:T(8,128)S(1)} %bitcast.12, f32[256,256]{1,0:T(8,128)S(1)} %bitcast.13, f32[256,256]{1,0:T(8,128)S(1)} %bitcast.14, f32[256,256]{1,0:T(8,128)S(1)} %bitcast.15, f32[256,256]{1,0:T(8,128)S(1)} %bitcast.16, ...), custom_call_target="tpu_custom_call" | custom-call | tf_op jit(solution)/shard_map/wave/pallas_call | solution.py:382
  34.6 0.7 %copy.16 = f32[16,16,256]{2,1,0:T(8,128)} copy(f32[16,16,256]{2,1,0:T(8,128)S(1)} %bitcast.11) | data formatting | bytes 524288
  35.3 0.7 %copy.17 = f32[16,16,256]{2,1,0:T(8,128)} copy(f32[16,16,256]{2,1,0:T(8,128)S(1)} %bitcast.10) | data formatting | bytes 524288
  36.0 0.7 %copy.18 = f32[16,16,256]{2,1,0:T(8,128)} copy(f32[16,16,256]{2,1,0:T(8,128)S(1)} %bitcast.9) | data formatting | bytes 524288
Async XLA Ops:
  0.6 0.7 %copy-start.9 = (f32[4,256]{1,0:T(4,128)S(1)}, f32[4,256]{1,0:T(4,128)}, u32[]{:S(2)}) copy-start(f32[4,256]{1,0:T(4,128)} %res.1) | copy-start | bytes 12292
  1.3 4.7 %copy-start.5 = (s32[3,16,1024]{2,1,0:T(8,128)S(1)}, s32[3,16,1024]{2,1,0:T(8,128)}, u32[]{:S(2)}) copy-start(s32[3,16,1024]{2,1,0:T(8,128)} %off_ref.1) | copy-start | bytes 589828
  1.3 4.7 %copy-start.6 = (f32[16,1024]{1,0:T(8,128)S(1)}, f32[16,1024]{1,0:T(8,128)}, u32[]{:S(2)}) copy-start(f32[16,1024]{1,0:T(8,128)} %w_ref.1) | copy-start | bytes 196612
  1.3 4.7 %copy-start.7 = (s32[3,1024]{1,0:T(4,128)S(1)}, s32[3,1024]{1,0:T(4,128)}, u32[]{:S(2)}) copy-start(s32[3,1024]{1,0:T(4,128)} %cell_ref.1) | copy-start | bytes 36868
  6.0 0.7 %copy-start.8 = (s32[1024]{0:T(1024)S(1)}, s32[1024]{0:T(1024)}, u32[]{:S(2)}) copy-start(s32[1024]{0:T(1024)} %param.19) | copy-start | bytes 12292
  6.7 2.3 %copy-start = (f32[16,16,256]{2,1,0:T(8,128)S(1)}, f32[16,16,256]{2,1,0:T(8,128)}, u32[]{:S(2)}) copy-start(f32[16,16,256]{2,1,0:T(8,128)} %param.10) | copy-start | bytes 786436
  6.7 2.3 %copy-start.1 = (f32[16,16,256]{2,1,0:T(8,128)S(1)}, f32[16,16,256]{2,1,0:T(8,128)}, u32[]{:S(2)}) copy-start(f32[16,16,256]{2,1,0:T(8,128)} %param.11) | copy-start | bytes 786436
  6.7 2.4 %copy-start.2 = (f32[16,16,256]{2,1,0:T(8,128)S(1)}, f32[16,16,256]{2,1,0:T(8,128)}, u32[]{:S(2)}) copy-start(f32[16,16,256]{2,1,0:T(8,128)} %param.12) | copy-start | bytes 786436
  6.7 2.4 %copy-start.3 = (f32[16,16,256]{2,1,0:T(8,128)S(1)}, f32[16,16,256]{2,1,0:T(8,128)}, u32[]{:S(2)}) copy-start(f32[16,16,256]{2,1,0:T(8,128)} %param.13) | copy-start | bytes 786436
  6.7 2.4 %copy-start.4 = (f32[16,16,256]{2,1,0:T(8,128)S(1)}, f32[16,16,256]{2,1,0:T(8,128)}, u32[]{:S(2)}) copy-start(f32[16,16,256]{2,1,0:T(8,128)} %param.14) | copy-start | bytes 786436
